TPU v7x, 32 devices: a whole 2x2x4 slice. The times are simulated.
32 devices in a mesh: seq: 16 (over z, x, core), head: 2 (over y).
Axes of the slice: x: 2, y: 2, z: 4, core: 2. Of those that a mesh axis runs over, the one named last changes fastest.
Arguments:
- query: bfloat16 [2048, 8192], P(('seq', 'head')), may hold values from -6 to 6
- key: bfloat16 [2048, 8192], P(('seq', 'head')), may hold values from -6 to 6
- value: bfloat16 [2048, 8192], P(('seq', 'head')), may hold values from -6 to 6
- cotangent: bfloat16 [2048, 8192], P(('seq', 'head')), may hold values from -6 to 6
- gain: float32 [8192], P('head'), may hold values from 0.5 to 1.5
- incoming_state: float32 [64, 128, 128], P('head'), may hold values from -288 to 288
Outputs:
- output: bfloat16 [2048, 8192], P(('seq', 'head'))
- grad_query: bfloat16 [2048, 8192], P(('seq', 'head'))
- grad_key: bfloat16 [2048, 8192], P(('seq', 'head'))
- grad_value: bfloat16 [2048, 8192], P(('seq', 'head'))
All inputs are finite; a program needn't handle non-finite values.
Results may differ from a plain program's by a relative error of at most 0.0058.
Values may be sent and summed in bfloat16 or wider, within the bound.
A program may use at most 128 MiB of HBM per device.

v0:
```python
import jax
import jax.numpy as jnp
from jax import lax
from jax.sharding import PartitionSpec as P

HEAD_DIM = 128


EPSILON = 1e-06


def prefix_2(part, axis, combine, identity, reverse):
    count = lax.axis_size(axis)
    place = lax.axis_index(axis)
    ahead = count - 1 - place if reverse else place
    gathered = lax.all_gather(part, axis)
    state = jnp.zeros_like(part) + jnp.asarray(identity, part.dtype)

    def one(step, state):
        source = count - 1 - step if reverse else step
        return combine(state, lax.dynamic_index_in_dim(gathered, source, 0, False))

    return lax.fori_loop(0, ahead, one, state)


def add_states(earlier, later):
    return earlier + later


def per_device(query, key, value, cotangent, gain, incoming_state):
    local_tokens = query.shape[0] * lax.axis_size("head")
    head_count = gain.shape[0] // HEAD_DIM
    query_local, key_local, value_local, upstream = (
        lax.all_to_all(query, "head", split_axis=1, concat_axis=0, tiled=True),
        lax.all_to_all(key, "head", split_axis=1, concat_axis=0, tiled=True),
        lax.all_to_all(value, "head", split_axis=1, concat_axis=0, tiled=True),
        lax.all_to_all(cotangent, "head", split_axis=1, concat_axis=0, tiled=True),
    )
    query_local = query_local.reshape(local_tokens, head_count, HEAD_DIM)
    key_local = key_local.reshape(local_tokens, head_count, HEAD_DIM)
    value_local = value_local.reshape(local_tokens, head_count, HEAD_DIM)
    causal = jnp.tril(jnp.ones((local_tokens, local_tokens), dtype=bool))[None]
    scores = jnp.einsum("thd,shd->hts", query_local, key_local, preferred_element_type=jnp.float32)
    weights = jnp.where(causal, scores, 0.0).astype(jnp.bfloat16)
    within = jnp.einsum("hts,she->the", weights, value_local, preferred_element_type=jnp.float32)
    block_state = jnp.einsum(
        "shd,she->hde", key_local, value_local, preferred_element_type=jnp.float32
    )
    prefix = prefix_2(block_state, "seq", add_states, jnp.zeros_like(block_state), False)
    states = (prefix + incoming_state).astype(jnp.bfloat16)
    attention = within + jnp.einsum(
        "thd,hde->the", query_local, states, preferred_element_type=jnp.float32
    )
    gain_rows = gain.reshape(head_count, HEAD_DIM)
    root_mean = jnp.sqrt(jnp.mean(attention * attention, axis=-1, keepdims=True) + EPSILON)
    normed = attention / root_mean
    output = (normed * gain_rows).astype(jnp.bfloat16).reshape(local_tokens, head_count * HEAD_DIM)
    upstream = upstream.reshape(local_tokens, head_count, HEAD_DIM)
    scaled = upstream.astype(jnp.float32) * gain_rows
    grad_attn = (
        (scaled - normed * jnp.mean(scaled * normed, axis=-1, keepdims=True)) / root_mean
    ).astype(jnp.bfloat16)
    grad_scores = jnp.where(
        causal,
        jnp.einsum("the,she->hts", grad_attn, value_local, preferred_element_type=jnp.float32),
        0.0,
    ).astype(jnp.bfloat16)
    grad_state = jnp.einsum(
        "thd,the->hde", query_local, grad_attn, preferred_element_type=jnp.float32
    )
    suffix = prefix_2(grad_state, "seq", add_states, jnp.zeros_like(grad_state), True)
    later_states = suffix.astype(jnp.bfloat16)
    grad_query = jnp.einsum(
        "hts,shd->thd", grad_scores, key_local, preferred_element_type=jnp.float32
    ) + jnp.einsum("the,hde->thd", grad_attn, states, preferred_element_type=jnp.float32)
    grad_key = jnp.einsum(
        "hts,thd->shd", grad_scores, query_local, preferred_element_type=jnp.float32
    ) + jnp.einsum("she,hde->shd", value_local, later_states, preferred_element_type=jnp.float32)
    grad_value = jnp.einsum(
        "hts,the->she", weights, grad_attn, preferred_element_type=jnp.float32
    ) + jnp.einsum("shd,hde->she", key_local, later_states, preferred_element_type=jnp.float32)
    flat_shape = (local_tokens, head_count * HEAD_DIM)
    grad_query = grad_query.astype(jnp.bfloat16).reshape(flat_shape)
    grad_key = grad_key.astype(jnp.bfloat16).reshape(flat_shape)
    grad_value = grad_value.astype(jnp.bfloat16).reshape(flat_shape)
    output, grad_query, grad_key, grad_value = (
        lax.all_to_all(output, "head", split_axis=0, concat_axis=1, tiled=True),
        lax.all_to_all(grad_query, "head", split_axis=0, concat_axis=1, tiled=True),
        lax.all_to_all(grad_key, "head", split_axis=0, concat_axis=1, tiled=True),
        lax.all_to_all(grad_value, "head", split_axis=0, concat_axis=1, tiled=True),
    )
    return (output, grad_query, grad_key, grad_value)


def solution(mesh):
    in_specs = (
        P(("seq", "head"), None),
        P(("seq", "head"), None),
        P(("seq", "head"), None),
        P(("seq", "head"), None),
        P("head"),
        P("head", None, None),
    )
    out_specs = (
        P(("seq", "head"), None),
        P(("seq", "head"), None),
        P(("seq", "head"), None),
        P(("seq", "head"), None),
    )
    return jax.shard_map(
        per_device, mesh=mesh, in_specs=in_specs, out_specs=out_specs, check_vma=False
    )
```

profile of v0, /device:TPU:1, one launch (start us, length us, event | category | flops | bytes accessed | tf_op | source)
XLA Modules:
  0.0 503.0 jit_solution(14681988587143458081)
XLA Ops:
  7.2 2.4 copy.171
  9.6 3.6 all-to-all-start.2
  14.2 12.8 %all-to-all-done.2 = bf16[64,2,4096]{2,0,1:T(8,128)(2,1)S(1)} async-done(((bf16[64,2,4096]{2,0,1:T(8,128)(2,1)}), bf16[64,2,4096]{2,0,1:T(8,128)(2,1)S(1)}, u32[]{:S(2)}, u32[]{:S(2)}) %all-to-all-start.2) | async-done | bytes 1048608 | tf_op jit(solution)/shard_map/all_to_all | solution.py:36
  27.0 3.6 all-to-all-start.1
  30.9 12.1 %all-to-all-done.1 = bf16[64,2,4096]{2,0,1:T(8,128)(2,1)S(1)} async-done(((bf16[64,2,4096]{2,0,1:T(8,128)(2,1)}), bf16[64,2,4096]{2,0,1:T(8,128)(2,1)S(1)}, u32[]{:S(2)}, u32[]{:S(2)}) %all-to-all-start.1) | async-done | bytes 1048608 | tf_op jit(solution)/shard_map/all_to_all | solution.py:35
  43.3 2.2 fusion.7
  47.8 3.6 all-to-all-start.4
  51.3 2.3 copy.173
  53.6 9.4 %all-to-all-done.4 = bf16[64,2,4096]{2,0,1:T(8,128)(2,1)S(1)} async-done(((bf16[64,2,4096]{2,0,1:T(8,128)(2,1)}), bf16[64,2,4096]{2,0,1:T(8,128)(2,1)S(1)}, u32[]{:S(2)}, u32[]{:S(2)}) %all-to-all-start.4) | async-done | bytes 1048608 | tf_op jit(solution)/shard_map/all_to_all | solution.py:37
  63.0 4.4 all-to-all-start
  69.4 3.0 copy.101
  72.4 6.0 %all-to-all-done = bf16[64,2,4096]{2,0,1:T(8,128)(2,1)} async-done(((bf16[64,2,4096]{2,0,1:T(8,128)(2,1)}), bf16[64,2,4096]{2,0,1:T(8,128)(2,1)}, u32[]{:S(2)}, u32[]{:S(2)}) %all-to-all-start) | async-done | bytes 1048608 | tf_op jit(solution)/shard_map/all_to_all | solution.py:34
  81.9 2.2 fusion.3
  84.1 131.7 %all-gather.5.cloned.1.call-done = f32[512,128,128]{2,1,0:T(8,128)} async-done(((f32[32,128,128]{2,1,0:T(8,128)}), f32[512,128,128]{2,1,0:T(8,128)}) %all-gather.5.cloned.1.call-update) | async-done | bytes 33554448 | tf_op jit(solution)/shard_map/all_gather | solution.py:16
  216.0 2.2 while.22
  216.0 2.1 bitcast_add_fusion.7
  218.2 2.0 add_convert_fusion.1
  225.1 2.1 convolution_bitcast_fusion
  227.2 2.9 copy.112
  233.3 4.6 all-to-all-start.3
  243.6 3.3 fusion.15
  246.9 3.4 all-to-all-done.3
  250.3 4.4 all-to-all-start.5
  254.7 173.6 %all-gather.7.cloned.1.call-done = f32[512,128,128]{2,1,0:T(8,128)} async-done(((f32[32,128,128]{2,1,0:T(8,128)}), f32[512,128,128]{2,1,0:T(8,128)}) %all-gather.7.cloned.1.call-update) | async-done | bytes 33554448 | tf_op jit(solution)/shard_map/all_gather | solution.py:16
  428.5 30.1 %while.23 = (s32[]{:T(128)}, f32[32,128,128]{2,1,0:T(8,128)S(1)}, s32[]{:T(128)}, f32[16,32,128,128]{3,2,1,0:T(8,128)}, s32[]{:T(128)}, /*index=5*/s32[]{:T(128)}, s32[]{:T(128)}, s32[]{:T(128)}) while((s32[]{:T(128)}, f32[32,128,128]{2,1,0:T(8,128)S(1)}, s32[]{:T(128)}, f32[16,32,128,128]{3,2,1,0:T(8,128)}, s32[]{:T(128)}, ...), condition=%wide.region_5.6_spmd, body=%wide.region_4.5_spmd.sunk | while | flops 524294 | bytes 6291599 | solution.py:23
  428.5 2.1 bitcast_add_fusion.8
  430.7 2.1 bitcast_add_fusion.8
  432.8 2.1 bitcast_add_fusion.8
  435.0 2.1 bitcast_add_fusion.8
  437.2 2.1 bitcast_add_fusion.8
  439.3 2.1 bitcast_add_fusion.8
  441.5 2.1 bitcast_add_fusion.8
  443.6 2.1 bitcast_add_fusion.8
  445.8 2.1 bitcast_add_fusion.8
  447.9 2.1 bitcast_add_fusion.8
  450.1 2.1 bitcast_add_fusion.8
  452.2 2.1 bitcast_add_fusion.8
  454.4 2.1 bitcast_add_fusion.8
  456.5 2.1 bitcast_add_fusion.8
  458.7 2.8 fusion
  463.1 2.3 all_to_all.121
  465.4 4.4 all-to-all-start.6
  476.7 4.4 all-to-all-done.6
  481.2 3.6 all-to-all-start.7
  484.7 2.3 copy.132
  487.0 2.3 copy.133
  489.3 2.3 copy.134
  491.6 3.5 all-to-all-done.7
  (66 shorter events, 33.0 us)
Async XLA Ops:
  7.2 6.0 %copy-start.13 = (bf16[64,8192]{1,0:T(8,128)(2,1)S(1)}, bf16[64,8192]{1,0:T(8,128)(2,1)}, u32[]{:S(2)}) copy-start(bf16[64,8192]{1,0:T(8,128)(2,1)} %param.11) | copy-start | bytes 3145732
  9.6 17.5 %all-to-all-start.2 = ((bf16[64,2,4096]{2,0,1:T(8,128)(2,1)}), bf16[64,2,4096]{2,0,1:T(8,128)(2,1)S(1)}, u32[]{:S(2)}, u32[]{:S(2)}) async-start(bf16[64,2,4096]{2,0,1:T(8,128)(2,1)} %bitcast.78), calls=%async_computation.2 | async-start | bytes 2097152 | tf_op jit(solution)/shard_map/all_to_all | solution.py:36
  27.0 16.0 %all-to-all-start.1 = ((bf16[64,2,4096]{2,0,1:T(8,128)(2,1)}), bf16[64,2,4096]{2,0,1:T(8,128)(2,1)S(1)}, u32[]{:S(2)}, u32[]{:S(2)}) async-start(bf16[64,2,4096]{2,0,1:T(8,128)(2,1)} %bitcast.79), calls=%async_computation.1 | async-start | bytes 2097152 | tf_op jit(solution)/shard_map/all_to_all | solution.py:35
  30.6 185.2 %all-gather.5.cloned.1.call-start = ((), (), s32[]{:S(2)}) async-start(), calls=%async_computation.8 | async-start | bytes 35651584 | tf_op jit(solution)/shard_map/all_gather | solution.py:16
  30.9 207.0 %copy-start.4 = (bf16[16,8,32,128]{3,2,1,0:T(8,128)(2,1)}, bf16[16,8,32,128]{3,2,1,0:T(8,128)(2,1)S(1)}, u32[]{:S(2)}) copy-start(bf16[16,8,32,128]{3,2,1,0:T(8,128)(2,1)S(1)} %copy.138) | copy-start | bytes 3145732
  43.3 36.6 %copy-start.1 = (bf16[16,8,32,128]{3,2,1,0:T(8,128)(2,1)}, bf16[16,8,32,128]{3,2,1,0:T(8,128)(2,1)S(1)}, u32[]{:S(2)}) copy-start(bf16[16,8,32,128]{3,2,1,0:T(8,128)(2,1)S(1)} %copy.137) | copy-start | bytes 3145732
  45.5 1.2 copy-start.14
  47.8 15.3 %all-to-all-start.4 = ((bf16[64,2,4096]{2,0,1:T(8,128)(2,1)}), bf16[64,2,4096]{2,0,1:T(8,128)(2,1)S(1)}, u32[]{:S(2)}, u32[]{:S(2)}) async-start(bf16[64,2,4096]{2,0,1:T(8,128)(2,1)} %bitcast.103), calls=%async_computation.4 | async-start | bytes 2097152 | tf_op jit(solution)/shard_map/all_to_all | solution.py:37
  63.0 15.3 %all-to-all-start = ((bf16[64,2,4096]{2,0,1:T(8,128)(2,1)}), bf16[64,2,4096]{2,0,1:T(8,128)(2,1)}, u32[]{:S(2)}, u32[]{:S(2)}) async-start(bf16[64,2,4096]{2,0,1:T(8,128)(2,1)} %bitcast.99), calls=%async_computation | async-start | bytes 2097152 | tf_op jit(solution)/shard_map/all_to_all | solution.py:34
  67.4 360.9 %all-gather.7.cloned.1.call-start = ((), (), s32[]{:S(2)}) async-start(), calls=%async_computation.9 | async-start | bytes 35651584 | tf_op jit(solution)/shard_map/all_gather | solution.py:16
  79.9 4.2 copy-start.5
  80.8 1.0 copy-start.11
  218.2 2.1 copy-start.6
  218.2 2.5 copy-start.10
  220.7 1.0 copy-start.8
  220.7 2.0 copy-start
  220.8 2.0 copy-start.15
  233.3 16.9 %all-to-all-start.3 = ((bf16[2,64,4096]{2,1,0:T(8,128)(2,1)}), bf16[2,64,4096]{2,1,0:T(8,128)(2,1)}, u32[]{:S(2)}, u32[]{:S(2)}) async-start(bf16[2,64,4096]{2,1,0:T(8,128)(2,1)} %all_to_all.111), calls=%async_computation.3 | async-start | bytes 2097152 | tf_op jit(solution)/shard_map/all_to_all | solution.py:87
  237.9 1.2 copy-start.2
  239.2 1.0 copy-start.12
  239.2 1.6 copy-start.9
  241.7 2.0 copy-start.7
  250.3 215.1 %all-to-all-start.5 = ((bf16[2,64,4096]{2,1,0:T(8,128)(2,1)}), bf16[2,64,4096]{2,1,0:T(8,128)(2,1)}, u32[]{:S(2)}, u32[]{:S(2)}) async-start(bf16[2,64,4096]{2,1,0:T(8,128)(2,1)} %all_to_all.117), calls=%async_computation.5 | async-start | bytes 2097152 | tf_op jit(solution)/shard_map/all_to_all | solution.py:88
  465.4 15.8 %all-to-all-start.6 = ((bf16[2,64,4096]{2,1,0:T(8,128)(2,1)}), bf16[2,64,4096]{2,1,0:T(8,128)(2,1)}, u32[]{:S(2)}, u32[]{:S(2)}) async-start(bf16[2,64,4096]{2,1,0:T(8,128)(2,1)} %all_to_all.121), calls=%async_computation.6 | async-start | bytes 2097152 | tf_op jit(solution)/shard_map/all_to_all | solution.py:89
  469.8 1.8 copy-start.3
  481.2 14.0 %all-to-all-start.7 = ((bf16[2,64,4096]{2,1,0:T(8,128)(2,1)}), bf16[2,64,4096]{2,1,0:T(8,128)(2,1)S(1)}, u32[]{:S(2)}, u32[]{:S(2)}) async-start(bf16[2,64,4096]{2,1,0:T(8,128)(2,1)} %all_to_all.125), calls=%async_computation.7 | async-start | bytes 2097152 | tf_op jit(solution)/shard_map/all_to_all | solution.py:90
Sparse Core Ops, SparseCore 0:
  45.6 170.1 all-gather.4
  230.2 198.0 all-gather.6
where the time goes:
time: 509 us; the launch traced here: 503 us
  waiting for transfers between devices  357 us (70%)
  local copies, waits for them, and re-layouts  41.9 us (8%)
  other arithmetic  36.6 us (7%)
  starting transfers between devices  32.2 us (6%)
  matrix products  20.6 us (4%)
  between operations  14.4 us (3%)
    all_gather x2, waiting for transfers between devices, prefix_2(): gathered = lax.all_gather(part, axis)  305 us
    add x15, other arithmetic, add_states(): return earlier + later  31.9 us
    all_to_all x1, waiting for transfers between devices, per_device(): lax.all_to_all(value, 'head', split_axis=1, concat_axis=0, tiled=True)  12.8 us
    all_to_all x1, waiting for transfers between devices, per_device(): lax.all_to_all(key, 'head', split_axis=1, concat_axis=0, tiled=True)  12.1 us
  transfers between devices with their start and end apart: 10, of which 9 were waited for; matrix products, arithmetic and copies ran while one was open for 14% of the time, Pallas kernels for 0%

commit v1 on v0

v1 whole, which is shorter than its diff:
```python
import functools

import jax
import jax.numpy as jnp
from jax import lax
from jax.experimental import pallas as pl
from jax.experimental.pallas import tpu as pltpu
from jax.sharding import PartitionSpec as P

HEAD_DIM = 128
EPSILON = 1e-06
MESH = pl.DeviceIdType.MESH
F32 = jnp.float32
BF16 = jnp.bfloat16

NT = (((1,), (1,)), ((), ()))
TN = (((0,), (0,)), ((), ()))
NN = (((1,), (0,)), ((), ()))


def dot(a, b, dims):
    return lax.dot_general(a, b, dims, preferred_element_type=F32)


def kernel(plan, q_hbm, k_hbm, v_hbm, y_hbm, gain_hbm, s0_hbm, o_hbm, gq_hbm, gk_hbm, gv_hbm,
           xin, xout, part, cum, gcum, pin, psend, sin, ssend, tot, gain,
           in_send, in_recv, out_send, out_recv, p_send, p_recv, s_send, s_recv, gain_sem):
    n_groups, sub, n_head, rows, heads, step = plan
    peers = sub * n_head
    chunks = heads // step
    block = rows * n_head
    width = heads * HEAD_DIM
    span = step * HEAD_DIM
    seq, hd = lax.axis_index("seq"), lax.axis_index("head")
    group, j = seq // sub, lax.rem(seq, sub)
    me = j * n_head + hd

    def place(p):
        other = lax.rem(me + p, peers)
        return other, (group * sub + other // n_head, lax.rem(other, n_head))

    def column(other, c):
        owner = lax.rem(other, n_head) * (sub * heads) + (other // n_head) * heads + c * step
        return pl.ds(pl.multiple_of(owner * HEAD_DIM, span), span)

    def strip(index):
        return pl.ds(pl.multiple_of(index * rows, rows), rows)

    later = (seq + sub, hd)
    earlier = (seq - sub, hd)
    barrier = pltpu.get_barrier_semaphore()

    def greet(p, carry):
        _, device = place(p)
        pl.semaphore_signal(barrier, inc=1, device_id=device, device_id_type=MESH)
        return carry

    lax.fori_loop(1, peers, greet, 0)

    @pl.when(group > 0)
    def _():
        pl.semaphore_signal(barrier, inc=1, device_id=earlier, device_id_type=MESH)

    @pl.when(group < n_groups - 1)
    def _():
        pl.semaphore_signal(barrier, inc=1, device_id=later, device_id_type=MESH)

    sources = ((k_hbm, v_hbm), (q_hbm, y_hbm))
    targets = ((o_hbm, gq_hbm), (gk_hbm, gv_hbm))

    for phase in range(2):
        for c in range(chunks):
            cols = pl.ds(c * span, span)
            for a in range(2):
                pltpu.make_async_copy(
                    sources[phase][a].at[:, column(me, c)],
                    xin.at[2 * phase + a, strip(me), cols],
                    in_recv.at[phase, c],
                ).start()

    gains = pltpu.make_async_copy(gain_hbm, gain, gain_sem)
    gains.start()

    @pl.when(group == 0)
    def _():
        for c in range(chunks):
            pltpu.make_async_copy(
                s0_hbm.at[pl.ds(j * heads + c * step, step)],
                pin.at[pl.ds(c * step, step)],
                p_recv.at[c],
            ).start()

    if n_groups == 1:
        pl.semaphore_wait(barrier, peers - 1)
    else:
        inner = jnp.logical_and(group > 0, group < n_groups - 1)

        @pl.when(inner)
        def _():
            pl.semaphore_wait(barrier, peers + 1)

        @pl.when(jnp.logical_not(inner))
        def _():
            pl.semaphore_wait(barrier, peers)

    for phase in range(2):
        for c in range(chunks):
            cols = pl.ds(c * span, span)

            def scatter(p, carry, phase=phase, c=c, cols=cols):
                other, device = place(p)
                for a in range(2):
                    pltpu.make_async_remote_copy(
                        src_ref=sources[phase][a].at[:, column(other, c)],
                        dst_ref=xin.at[2 * phase + a, strip(me), cols],
                        send_sem=in_send.at[phase, c],
                        recv_sem=in_recv.at[phase, c],
                        device_id=device,
                        device_id_type=MESH,
                    ).start()
                return carry

            lax.fori_loop(1, peers, scatter, 0)

    def arrived(phase, c):
        ref = xin.at[pl.ds(2 * phase, 2), :, pl.ds(c * span, span)]
        pltpu.make_async_copy(ref, ref, in_recv.at[phase, c]).wait()

    def give(phase, c):
        cols = pl.ds(c * span, span)

        def back(p, carry):
            other, device = place(p)
            for a in range(2):
                pltpu.make_async_remote_copy(
                    src_ref=xout.at[2 * phase + a, strip(other), cols],
                    dst_ref=targets[phase][a].at[:, column(me, c)],
                    send_sem=out_send.at[phase, c],
                    recv_sem=out_recv.at[phase, c],
                    device_id=device,
                    device_id_type=MESH,
                ).start()
            return carry

        lax.fori_loop(1, peers, back, 0)
        for a in range(2):
            pltpu.make_async_copy(
                xout.at[2 * phase + a, strip(me), cols],
                targets[phase][a].at[:, column(me, c)],
                out_recv.at[phase, c],
            ).start()

    def state_copy(src, dst, send, recv, c, device):
        piece = pl.ds(c * step, step)
        return pltpu.make_async_remote_copy(
            src_ref=src.at[piece], dst_ref=dst.at[piece], send_sem=send.at[c],
            recv_sem=recv.at[c], device_id=device, device_id_type=MESH)

    def pass_prefix(c):
        piece = pl.ds(c * step, step)
        pltpu.make_async_copy(pin.at[piece], pin.at[piece], p_recv.at[c]).wait()

        @pl.when(group < n_groups - 1)
        def _():
            psend[c * step:(c + 1) * step] = (
                pin[c * step:(c + 1) * step] + tot[c * step:(c + 1) * step])
            state_copy(psend, pin, p_send, p_recv, c, later).start()

    for c in range(chunks):
        arrived(0, c)
        for h in range(c * step, (c + 1) * step):
            hc = slice(h * HEAD_DIM, (h + 1) * HEAD_DIM)
            run = jnp.zeros((HEAD_DIM, HEAD_DIM), F32)
            for b in range(sub):
                r = slice(b * block, (b + 1) * block)
                cum[h, b] = run
                run = run + dot(xin[0, r, hc], xin[1, r, hc], TN)
            tot[h] = run

        @pl.when(group == 0)
        def _(c=c):
            pass_prefix(c)

    row = lax.broadcasted_iota(jnp.int32, (block, block), 0)
    col = lax.broadcasted_iota(jnp.int32, (block, block), 1)
    causal = col <= row
    gains.wait()

    for c in range(chunks):
        @pl.when(group > 0)
        def _(c=c):
            pass_prefix(c)

    for c in range(chunks):
        arrived(1, c)
        for h in range(c * step, (c + 1) * step):
            hc = slice(h * HEAD_DIM, (h + 1) * HEAD_DIM)
            g = gain[pl.ds(j * heads + h, 1), :]
            carried = pin[h]
            run = jnp.zeros((HEAD_DIM, HEAD_DIM), F32)
            for b in reversed(range(sub)):
                r = slice(b * block, (b + 1) * block)
                k, v, q, up = xin[0, r, hc], xin[1, r, hc], xin[2, r, hc], xin[3, r, hc]
                state = (carried + cum[h, b]).astype(BF16)
                w = jnp.where(causal, dot(q, k, NT), 0.0).astype(BF16)
                att = dot(w, v, NN) + dot(q, state, NN)
                inv = lax.rsqrt(jnp.mean(att * att, axis=-1, keepdims=True) + EPSILON)
                normed = att * inv
                xout[0, r, hc] = (normed * g).astype(BF16)
                scaled = up.astype(F32) * g
                ga = ((scaled - normed * jnp.mean(scaled * normed, axis=-1, keepdims=True))
                      * inv).astype(BF16)
                gw = jnp.where(causal, dot(ga, v, NT), 0.0).astype(BF16)
                xout[1, r, hc] = (dot(gw, k, NN) + dot(ga, state, NT)).astype(BF16)
                part[0, r, hc] = dot(gw, q, TN)
                part[1, r, hc] = dot(w, ga, TN)
                gcum[h, b] = run
                run = run + dot(q, ga, TN)
            tot[h] = run

        @pl.when(jnp.logical_and(group == n_groups - 1, group > 0))
        def _(c=c):
            ssend[c * step:(c + 1) * step] = tot[c * step:(c + 1) * step]
            state_copy(ssend, sin, s_send, s_recv, c, earlier).start()

        give(0, c)

    for c in range(chunks):
        piece = pl.ds(c * step, step)

        @pl.when(group == n_groups - 1)
        def _(c=c):
            sin[c * step:(c + 1) * step] = jnp.zeros((step, HEAD_DIM, HEAD_DIM), F32)

        @pl.when(group < n_groups - 1)
        def _(c=c, piece=piece):
            pltpu.make_async_copy(sin.at[piece], sin.at[piece], s_recv.at[c]).wait()

            @pl.when(group > 0)
            def _():
                ssend[c * step:(c + 1) * step] = (
                    sin[c * step:(c + 1) * step] + tot[c * step:(c + 1) * step])
                state_copy(ssend, sin, s_send, s_recv, c, earlier).start()

        for h in range(c * step, (c + 1) * step):
            hc = slice(h * HEAD_DIM, (h + 1) * HEAD_DIM)
            after = sin[h]
            for b in range(sub):
                r = slice(b * block, (b + 1) * block)
                suffix = (after + gcum[h, b]).astype(BF16)
                xout[2, r, hc] = (part[0, r, hc] + dot(xin[1, r, hc], suffix, NT)).astype(BF16)
                xout[3, r, hc] = (part[1, r, hc] + dot(xin[0, r, hc], suffix, NN)).astype(BF16)
        give(1, c)

    for phase in range(2):
        for c in range(chunks):
            sent = xin.at[pl.ds(2 * phase, 2), pl.ds(0, (peers - 1) * rows), pl.ds(c * span, span)]
            pltpu.make_async_copy(sent, sent, in_send.at[phase, c]).wait()
            pltpu.make_async_copy(sent, sent, out_send.at[phase, c]).wait()
            whole = xout.at[pl.ds(2 * phase, 2), :, pl.ds(c * span, span)]
            pltpu.make_async_copy(whole, whole, out_recv.at[phase, c]).wait()
    for c in range(chunks):
        @pl.when(group < n_groups - 1)
        def _(c=c):
            state_copy(psend, pin, p_send, p_recv, c, later).wait_send()

        @pl.when(group > 0)
        def _(c=c):
            state_copy(ssend, sin, s_send, s_recv, c, earlier).wait_send()


def per_device(mesh, query, key, value, cotangent, gain, incoming_state):
    n_seq, n_head = mesh.shape["seq"], mesh.shape["head"]
    rows, features = query.shape
    local_heads = incoming_state.shape[0]
    sub = 1
    while sub < 4 and n_seq % (2 * sub) == 0 and local_heads % (2 * sub) == 0:
        sub *= 2
    heads = local_heads // sub
    step = max(1, heads // 4)
    chunks = heads // step
    tokens = rows * n_head * sub
    width = heads * HEAD_DIM
    plan = (n_seq // sub, sub, n_head, rows, heads, step)
    anywhere = pl.BlockSpec(memory_space=pl.ANY)
    resident = pl.BlockSpec(memory_space=pltpu.HBM)
    state = pltpu.VMEM((heads, HEAD_DIM, HEAD_DIM), F32)
    states = pltpu.VMEM((heads, sub, HEAD_DIM, HEAD_DIM), F32)
    sems = pltpu.SemaphoreType.DMA((2, chunks))
    chain = pltpu.SemaphoreType.DMA((chunks,))
    return pl.pallas_call(
        functools.partial(kernel, plan),
        out_shape=[jax.ShapeDtypeStruct((rows, features), BF16)] * 4,
        in_specs=[resident] * 6,
        out_specs=[anywhere] * 4,
        scratch_shapes=[
            pltpu.VMEM((4, tokens, width), BF16),
            pltpu.VMEM((4, tokens, width), BF16),
            pltpu.VMEM((2, tokens, width), F32),
            states, states, state, state, state, state, state,
            pltpu.VMEM((local_heads, HEAD_DIM), F32),
            sems, sems, sems, sems, chain, chain, chain, chain,
            pltpu.SemaphoreType.DMA,
        ],
        compiler_params=pltpu.CompilerParams(
            collective_id=0, has_side_effects=True, vmem_limit_bytes=48 * 1024 * 1024),
    )(query, key, value, cotangent, gain.reshape(local_heads, HEAD_DIM), incoming_state)


def solution(mesh):
    tokens = P(("seq", "head"), None)
    return jax.shard_map(
        functools.partial(per_device, mesh),
        mesh=mesh,
        in_specs=(tokens, tokens, tokens, tokens, P("head"), P("head", None, None)),
        out_specs=(tokens, tokens, tokens, tokens),
        check_vma=False,
    )
```

time: 509 us -> 102 us (0.20); the launches traced: 503 us -> 102 us
  waiting for transfers between devices: 357 us -> 0 us
  Pallas kernels: 0 us -> 95.3 us
  other arithmetic: 36.6 us -> 0 us
  local copies, waits for them, and re-layouts: 41.9 us -> 5.82 us
  starting transfers between devices: 32.2 us -> 0 us
  matrix products: 20.6 us -> 0 us
  between operations: 14.4 us -> 0.65 us
    all_gather x2 -> x0, waiting for transfers between devices: 305 us -> none  [prefix_2(): gathered = lax.all_gather(part, axis)]
    pallas_call x0 -> x1, Pallas kernels: none -> 95.3 us  [per_device(): pl.pallas_call(functools.partial(kernel, plan), out_shape=[jax.ShapeDtype...]
    all_to_all x8 -> x0, waiting for transfers between devices: 51.6 us -> none  [the longest x1 12.8 us: per_device(): lax.all_to_all(value, 'head', split_axis=1, concat_axis=0, tiled=True)]
    all_to_all x8 -> x0, starting transfers between devices: 32.2 us -> none  [the longest x1 4.6 us: per_device(): lax.all_to_all(output, 'head', split_axis=0, concat_axis=1, tiled=True)]
    add x15 -> x0, other arithmetic: 31.9 us -> none  [add_states(): return earlier + later]
    all_to_all x12 -> x0, local copies, waits for them, and re-layouts: 20.8 us -> none  [the longest x2 4.58 us: per_device(): lax.all_to_all(grad_key, 'head', split_axis=0, concat_axis=1, tiled=True)]
    dot_general x12 -> x0, matrix products: 20.6 us -> none  [the longest x1 3.25 us: per_device(): jnp.einsum('hts,thd->shd', grad_scores, query_local, preferred_element_ty...]
    convert_element_type x5 -> x0, local copies, waits for them, and re-layouts: 9.17 us -> none  [the longest x1 2.99 us: per_device(): scaled = upstream.astype(jnp.float32) * gain_rows]
  transfers between devices with their start and end apart: 10 -> 0, of which waited for: 9 -> 0; matrix products, arithmetic and copies ran while one was open for 14% -> 0% of each run, Pallas kernels for 0% -> 0%
where the time goes in v1:
time: 102 us
  Pallas kernels  95.3 us (93%)
  local copies, waits for them, and re-layouts  5.82 us (6%)
    pallas_call x1, Pallas kernels, per_device(): pl.pallas_call(functools.partial(kernel, plan), out_shape=[jax.ShapeDtype...  95.3 us
    unnamed x8, local copies, waits for them, and re-layouts  5.82 us

profile of v1, /device:TPU:1, one launch (start us, length us, event | category | flops | bytes accessed | tf_op | source)
XLA Modules:
  0.0 101.8 jit_solution(5439615589069733288)
XLA Ops:
  0.6 0.0 copy-start
  0.6 1.2 %copy-done = bf16[64,8192]{1,0:T(8,128)(2,1)S(1)} copy-done((bf16[64,8192]{1,0:T(8,128)(2,1)S(1)}, bf16[64,8192]{1,0:T(8,128)(2,1)}, u32[]{:S(2)}) %copy-start) | copy-done | bytes 1048600
  1.9 0.0 copy-start.1
  1.9 0.7 copy-done.1
  2.6 95.3 %shard_map.93 = (bf16[64,8192]{1,0:T(8,128)(2,1)S(1)}, bf16[64,8192]{1,0:T(8,128)(2,1)S(1)}, bf16[64,8192]{1,0:T(8,128)(2,1)S(1)}, bf16[64,8192]{1,0:T(8,128)(2,1)S(1)}) custom-call(bf16[64,8192]{1,0:T(8,128)(2,1)S(1)} %copy-done, bf16[64,8192]{1,0:T(8,128)(2,1)} %k_hbm.1, bf16[64,8192]{1,0:T(8,128)(2,1)} %v_hbm.1, bf16[64,8192]{1,0:T(8,128)(2,1)} %y_hbm.1, ...), custom_call_target="tpu_custom_call" | custom-call | tf_op jit(solution)/shard_map/pallas_call | solution.py:291
  97.9 1.0 copy.14
  98.9 1.0 copy.15
  99.8 1.0 copy.16
  100.8 1.0 copy.17
Async XLA Ops:
  0.6 1.2 %copy-start = (bf16[64,8192]{1,0:T(8,128)(2,1)S(1)}, bf16[64,8192]{1,0:T(8,128)(2,1)}, u32[]{:S(2)}) copy-start(bf16[64,8192]{1,0:T(8,128)(2,1)} %q_hbm.1) | copy-start | bytes 3145732
  1.9 0.7 copy-start.1

commit v2 on v1

--- a/solution.py
+++ b/solution.py
@@ -303,7 +303,7 @@
             pltpu.SemaphoreType.DMA,
         ],
         compiler_params=pltpu.CompilerParams(
-            collective_id=0, has_side_effects=True, vmem_limit_bytes=48 * 1024 * 1024),
+            collective_id=0, has_side_effects=True, vmem_limit_bytes=51000 * 1024),
     )(query, key, value, cotangent, gain.reshape(local_heads, HEAD_DIM), incoming_state)
 
 

time: 102 us -> 101 us (level)
  local copies, waits for them, and re-layouts: 5.82 us -> 4.59 us
    unnamed x8 -> x6, local copies, waits for them, and re-layouts: 5.82 us -> 4.59 us
where the time goes in v2:
time: 101 us
  Pallas kernels  95.3 us (94%)
  local copies, waits for them, and re-layouts  4.59 us (5%)
    pallas_call x1, Pallas kernels, per_device(): pl.pallas_call(functools.partial(kernel, plan), out_shape=[jax.ShapeDtype...  95.3 us
    unnamed x6, local copies, waits for them, and re-layouts  4.59 us

profile of v2, /device:TPU:1, one launch (start us, length us, event | category | flops | bytes accessed | tf_op | source)
XLA Modules:
  0.0 100.6 jit_solution(7546822344428470009)
XLA Ops:
  0.6 0.0 copy-start
  0.6 0.7 copy-done
  1.4 95.3 %shard_map.93 = (bf16[64,8192]{1,0:T(8,128)(2,1)S(1)}, bf16[64,8192]{1,0:T(8,128)(2,1)S(1)}, bf16[64,8192]{1,0:T(8,128)(2,1)S(1)}, bf16[64,8192]{1,0:T(8,128)(2,1)S(1)}) custom-call(bf16[64,8192]{1,0:T(8,128)(2,1)} %q_hbm.1, bf16[64,8192]{1,0:T(8,128)(2,1)} %k_hbm.1, bf16[64,8192]{1,0:T(8,128)(2,1)} %v_hbm.1, bf16[64,8192]{1,0:T(8,128)(2,1)} %y_hbm.1, ...), custom_call_target="tpu_custom_call" | custom-call | tf_op jit(solution)/shard_map/pallas_call | solution.py:291
  96.7 1.0 copy.14
  97.7 1.0 copy.15
  98.6 1.0 copy.16
  99.6 1.0 copy.17
Async XLA Ops:
  0.6 0.7 copy-start
